TPU v7x, 512 devices: a whole 4x8x8 slice. The times are simulated.
512 devices in a mesh: batch: 128 (over x, z, y_hi), mp: 4 (over y_lo, core).
Axes of the slice: x: 4, y: 8 (y_hi: 4, y_lo: 2; y = y_hi * 2 + y_lo), z: 8, core: 2. Of those that a mesh axis runs over, the one named last changes fastest.
Arguments:
- query_hidden: bfloat16 [131072, 768], P(('batch', 'mp')), may hold values from -28 to 28
- passage_hidden: bfloat16 [655360, 768], P(('batch', 'mp')), may hold values from -28 to 28
- projection: bfloat16 [768, 128], replicated, may hold values from -0.21875 to 0.21875
- query_lengths: int32 [4096], P(('batch', 'mp')), may hold values from 8 to 32, as said below
- passage_lengths: int32 [5120], P(('batch', 'mp')), may hold values from 64 to 128, as said below
- positives: int32 [4096], P(('batch', 'mp')), may hold values from 0 to 9
Outputs:
- query_loss: float32 [4096], P(('batch', 'mp'))
- grad_query_hidden: bfloat16 [131072, 768], P(('batch', 'mp'))
- grad_passage_hidden: bfloat16 [655360, 768], P(('batch', 'mp'))
- grad_projection: float32 [768, 128], replicated
Inputs may be any that keep to these rules, and one draw needn't show every extreme that they name: `query_lengths`: the first query of each block of 8 queries has all 32 tokens. `passage_lengths`: the first passage of each block of 10 passages has all 128 tokens.
All inputs are finite; a program needn't handle non-finite values.
Results may differ from a plain program's by a relative error of at most 0.012.
The roundings to bfloat16 on the way count: a program that leaves them out, or rounds other values in their place, can miss the bound.
Values may be sent and summed in bfloat16 or wider, within the bound.
A program may use at most 64 MiB of HBM per device.

v0:
```python
import jax
import jax.numpy as jnp
from jax import lax
from jax.sharding import PartitionSpec as P

inner_scale = 128.0
outer_scale = 8.0
loss_scale = 32.0
norm_eps = 1e-06


def shifted(block, axis, distance):
    devices = range(lax.axis_size(axis))
    route = [((i - distance) % len(devices), i) for i in devices]
    return lax.ppermute(block, axis, route)


def embed_rows(hidden, projection):
    before = jnp.dot(hidden, projection, preferred_element_type=jnp.float32)
    radius = jnp.sqrt(jnp.sum(before * before, axis=-1, keepdims=True) + norm_eps)
    return (before / radius, radius)


def candidate_block(query_embed, passage_embed, passage_valid, query_keep):
    queries, query_tokens = query_keep.shape
    passages, passage_tokens = passage_valid.shape
    sims = jnp.dot(query_embed, passage_embed.T, preferred_element_type=jnp.float32)
    sims = sims.reshape(queries, query_tokens, passages, passage_tokens)
    logits = jnp.where(passage_valid[None, None], sims * inner_scale, -jnp.inf)
    row_top = jnp.max(logits, axis=-1, keepdims=True)
    powers = jnp.exp(logits - row_top)
    totals = jnp.sum(powers, axis=-1, keepdims=True)
    weights = powers / totals
    best = (jnp.log(totals[..., 0]) + row_top[..., 0]) / inner_scale
    scores = outer_scale * jnp.sum(query_keep[:, :, None] * best, axis=1)
    return (scores, weights)


def softmax_loss(scores, positives):
    row_top = jnp.max(scores, axis=1, keepdims=True)
    totals = jnp.sum(jnp.exp(scores - row_top), axis=1, keepdims=True)
    log_total = row_top + jnp.log(totals)
    probs = jnp.exp(scores - log_total)
    columns = jnp.arange(scores.shape[1], dtype=jnp.int32)
    onehot = (columns[None, :] == positives[:, None]).astype(jnp.float32)
    losses = log_total[:, 0] - jnp.sum(onehot * scores, axis=1)
    return (losses, loss_scale * (probs - onehot))


def block_grads(dscores, query_keep, weights, query_embed, passage_embed):
    grad_sim = (
        outer_scale * dscores[:, None, :, None] * query_keep[:, :, None, None] * weights
    ).astype(jnp.bfloat16)
    flat = grad_sim.reshape(query_embed.shape[0], passage_embed.shape[0])
    to_query = jnp.dot(flat, passage_embed, preferred_element_type=jnp.float32)
    to_passage = lax.dot_general(
        flat, query_embed, (((0,), (0,)), ((), ())), preferred_element_type=jnp.float32
    )
    return (to_query, to_passage)


def back_norm(grad, unit, radius):
    return ((grad - unit * jnp.sum(unit * grad, axis=-1, keepdims=True)) / radius).astype(
        jnp.bfloat16
    )


def contract_rows(left, right):
    return lax.dot_general(
        left, right, (((0,), (0,)), ((), ())), preferred_element_type=jnp.float32
    )


def per_device(query_hidden, passage_hidden, projection, query_lengths, passage_lengths, positives):
    queries = query_lengths.shape[0]
    passages = passage_lengths.shape[0]
    query_tokens = query_hidden.shape[0] // queries
    passage_tokens = passage_hidden.shape[0] // passages
    query_unit, query_radius = embed_rows(query_hidden, projection)
    passage_unit, passage_radius = embed_rows(passage_hidden, projection)
    query_embed = query_unit.astype(jnp.bfloat16)
    passage_embed = passage_unit.astype(jnp.bfloat16)
    length_values = passage_lengths.astype(jnp.bfloat16)
    query_keep = (
        jnp.arange(query_tokens, dtype=jnp.int32)[None, :] < query_lengths[:, None]
    ).astype(jnp.float32)
    slots = jnp.arange(passage_tokens, dtype=jnp.float32)
    members = [(passage_embed, length_values)]
    current = (passage_embed, length_values)
    for repeat in range(2):
        current = shifted((current[0], current[1]), "batch", -1)
        members.append(current)
    score_list = []
    weight_list = []
    for member in members:
        valid = slots[None, :] < member[1].astype(jnp.float32)[:, None]
        scores, weights = candidate_block(query_embed, member[0], valid, query_keep)
        score_list.append(scores)
        weight_list.append(weights)
    losses, dscores = softmax_loss(jnp.concatenate(score_list, axis=1), positives)
    query_grad = jnp.zeros(query_unit.shape, jnp.float32)
    passage_terms = []
    for column in range(3):
        to_query, to_passage = block_grads(
            dscores[:, column * passages : (column + 1) * passages],
            query_keep,
            weight_list[column],
            query_embed,
            members[column][0],
        )
        query_grad = query_grad + to_query
        passage_terms.append(to_passage)
    query_pre_grad = back_norm(query_grad, query_unit, query_radius)
    query_partial = contract_rows(query_hidden, query_pre_grad)
    carried = passage_terms[2]
    for repeat in range(2):
        carried = (
            shifted(carried.astype(jnp.bfloat16), "batch", 1).astype(carried.dtype)
            + passage_terms[1 - repeat]
        )
    passage_pre_grad = back_norm(carried, passage_unit, passage_radius)
    grad_query_hidden = jnp.dot(
        query_pre_grad, projection.T, preferred_element_type=jnp.float32
    ).astype(jnp.bfloat16)
    grad_passage_hidden = jnp.dot(
        passage_pre_grad, projection.T, preferred_element_type=jnp.float32
    ).astype(jnp.bfloat16)
    passage_partial = contract_rows(passage_hidden, passage_pre_grad)
    weight_total = lax.psum(query_partial + passage_partial, ("batch", "mp"))
    grad_projection = weight_total / (lax.axis_size("batch") * lax.axis_size("mp"))
    return (losses, grad_query_hidden, grad_passage_hidden, grad_projection)


def solution(mesh):
    in_specs = (
        P(("batch", "mp"), None),
        P(("batch", "mp"), None),
        P(),
        P(("batch", "mp")),
        P(("batch", "mp")),
        P(("batch", "mp")),
    )
    out_specs = (P(("batch", "mp")), P(("batch", "mp"), None), P(("batch", "mp"), None), P())
    return jax.shard_map(
        per_device, mesh=mesh, in_specs=in_specs, out_specs=out_specs, check_vma=False
    )
```

profile of v0, /device:TPU:1, one launch (start us, length us, event | category | flops | bytes accessed | tf_op | source)
XLA Modules:
  0.0 411.5 jit_solution(9129074453687419694)
XLA Ops:
  7.3 1.5 copy-done
  8.7 1.7 multiply_reduce_fusion.1
  10.5 0.9 fusion.16
  11.4 17.4 %collective-permute-start.1 = (bf16[1280,128]{0,1:T(8,128)(2,1)}, bf16[1280,128]{0,1:T(8,128)(2,1)}, u32[]{:S(2)}, u32[]{:S(2)}) collective-permute-start(bf16[1280,128]{0,1:T(8,128)(2,1)} %fusion.16), channel_id=1, source_target_pairs={{4,0},{8,4},{12,8},{16,12},{20,16},{24,20},{28,24},{32,28},{36,32}... | collective-permute-start | bytes 983048 | tf_op jit(solution)/shard_map/ppermute | solution.py:15
  28.8 0.5 convert_convert_fusion
  29.3 3.8 collective-permute-start
  33.0 0.7 fusion.11
  33.7 0.7 fusion.10
  34.4 0.7 iota_compare_fusion.2
  35.1 0.3 multiply_reduce_fusion.6
  35.5 0.6 copy-done.15
  36.1 1.3 convolution_multiply_fusion.2
  37.5 1.6 mul.189
  39.0 2.4 select_reduce_fusion.2
  41.4 2.0 exponential_reduce_fusion.2
  43.4 0.6 bitcast_compare_fusion.2
  44.0 0.6 convert_element_type.72
  44.8 0.6 bitcast_compare_fusion.1
  45.4 9.0 %collective-permute-start.2 = (bf16[10]{0:T(256)(128)(2,1)}, bf16[10]{0:T(256)(128)(2,1)S(1)}, u32[]{:S(2)}, u32[]{:S(2)}) collective-permute-start(bf16[10]{0:T(256)(128)(2,1)} %collective-permute-done), channel_id=1, source_target_pairs={{4,0},{8,4},{12,8},{16,12},{20,16},{24,20},{28,24},{32,28},{36,32}... | collective-permute-start | bytes 68 | tf_op jit(solution)/shard_map/ppermute | solution.py:15
  54.4 0.8 collective-permute-done.2
  55.3 0.6 bitcast_compare_fusion
  55.9 2.4 convolution_multiply_fusion.1
  58.3 2.7 mul.196
  60.9 10.2 %collective-permute-start.3 = (bf16[1280,128]{0,1:T(8,128)(2,1)}, bf16[1280,128]{0,1:T(8,128)(2,1)S(1)}, u32[]{:S(2)}, u32[]{:S(2)}) collective-permute-start(bf16[1280,128]{0,1:T(8,128)(2,1)} %collective-permute-done.1), channel_id=1, source_target_pairs={{4,0},{8,4},{12,8},{16,12},{20,16},{24,20},{28,24},{32,28},{36,32}... | collective-permute-start | bytes 983048 | tf_op jit(solution)/shard_map/ppermute | solution.py:15
  71.2 2.2 select_reduce_fusion.1
  73.4 1.9 exponential_reduce_fusion.1
  75.4 1.1 collective-permute-done.3
  76.5 0.7 copy-done.19
  77.2 1.4 convolution_multiply_fusion
  78.7 2.7 mul.200
  81.3 2.4 select_reduce_fusion
  83.7 1.3 exponential_reduce_fusion
  85.5 0.2 select_reduce_fusion.3
  85.7 0.5 fusion.17
  86.5 0.6 div.74
  87.2 0.6 sub.67
  87.8 0.6 mul.210
  88.4 2.0 fusion.7
  90.4 1.3 fusion.18
  91.7 0.6 div.80
  92.4 0.6 sub.71
  93.0 0.6 mul.222
  93.7 2.0 fusion.1
  95.7 0.3 convolution_convert_fusion.1
  95.9 3.1 collective-permute-start.4
  99.0 0.6 div.77
  99.6 0.6 sub.69
  100.2 0.6 mul.216
  100.9 2.0 fusion.4
  102.9 1.3 convolution_add_fusion.2
  104.3 0.4 multiply_reduce_fusion.2
  104.8 5.4 %collective-permute-done.4 = bf16[1280,128]{0,1:T(8,128)(2,1)S(1)} collective-permute-done((bf16[1280,128]{0,1:T(8,128)(2,1)S(1)}, bf16[1280,128]{0,1:T(8,128)(2,1)S(1)}, u32[]{:S(2)}, u32[]{:S(2)}) %collective-permute-start.4) | collective-permute-done | bytes 327712 | tf_op jit(solution)/shard_map/ppermute | solution.py:15
  110.2 0.3 add_convert_fusion
  110.4 1.9 collective-permute-start.5
  112.3 1.0 convolution_convert_fusion.2
  113.4 0.2 fusion.19
  113.6 13.6 %collective-permute-done.5 = bf16[1280,128]{0,1:T(8,128)(2,1)S(1)} collective-permute-done((bf16[1280,128]{0,1:T(8,128)(2,1)S(1)}, bf16[1280,128]{0,1:T(8,128)(2,1)S(1)}, u32[]{:S(2)}, u32[]{:S(2)}) %collective-permute-start.5) | collective-permute-done | bytes 327712 | tf_op jit(solution)/shard_map/ppermute | solution.py:15
  127.2 0.3 multiply_reduce_fusion
  127.5 0.1 divide_convert_fusion
  127.6 1.2 fusion.9
  128.8 2.0 convolution_convert_fusion
  130.8 271.9 %all-reduce.2.cloned.1.call-done = f32[768,128]{0,1:T(8,128)} async-done(((f32[768,128]{0,1:T(8,128)}), f32[768,128]{0,1:T(8,128)}) %all-reduce.2.cloned.1.call-update) | async-done | bytes 393232 | tf_op jit(solution)/shard_map/psum | solution.py:129
  402.7 1.0 broadcast_multiply_fusion
  403.8 0.9 copy.15
  (82 shorter events, 1.5 us)
Async XLA Ops:
  7.2 1.6 copy-start
  7.2 27.9 %copy-start.8 = (bf16[768,128]{1,0:T(8,128)(2,1)S(1)}, bf16[768,128]{1,0:T(8,128)(2,1)}, u32[]{:S(2)}) copy-start(bf16[768,128]{1,0:T(8,128)(2,1)} %param.8) | copy-start | bytes 589828
  7.2 21.6 %copy-start.31 = (s32[10]{0:T(128)S(1)}, s32[10]{0:T(128)}, u32[]{:S(2)}) copy-start(s32[10]{0:T(128)} %param.10) | copy-start | bytes 124
  7.2 25.8 %copy-start.29 = (s32[8]{0:T(128)S(1)}, s32[8]{0:T(128)}, u32[]{:S(2)}) copy-start(s32[8]{0:T(128)} %param.9) | copy-start | bytes 100
  7.2 27.9 %copy-start.13 = (bf16[256,768]{1,0:T(8,128)(2,1)S(1)}, bf16[256,768]{1,0:T(8,128)(2,1)}, u32[]{:S(2)}) copy-start(bf16[256,768]{1,0:T(8,128)(2,1)} %param.6) | copy-start | bytes 1179652
  7.2 395.5 %all-reduce.2.cloned.1.call-start = ((), (), s32[]{:S(2)}) async-start(), calls=%async_computation | async-start | bytes 786432 | tf_op jit(solution)/shard_map/psum | solution.py:129
  10.5 25.0 %copy-start.6 = (f32[1280,128]{0,1:T(8,128)}, f32[1280,128]{0,1:T(8,128)S(1)}, u32[]{:S(2)}) copy-start(f32[1280,128]{0,1:T(8,128)S(1)} %get-tuple-element.37) | copy-start | bytes 1966084
  11.4 44.5 %collective-permute-start.1 = (bf16[1280,128]{0,1:T(8,128)(2,1)}, bf16[1280,128]{0,1:T(8,128)(2,1)}, u32[]{:S(2)}, u32[]{:S(2)}) collective-permute-start(bf16[1280,128]{0,1:T(8,128)(2,1)} %fusion.16), channel_id=1, source_target_pairs={{4,0},{8,4},{12,8},{16,12},{20,16},{24,20},{28,24},{32,28},{36,32}... | collective-permute-start | bytes 983048 | tf_op jit(solution)/shard_map/ppermute | solution.py:15
  29.3 14.7 %collective-permute-start = (bf16[10]{0:T(256)(128)(2,1)}, bf16[10]{0:T(256)(128)(2,1)}, u32[]{:S(2)}, u32[]{:S(2)}) collective-permute-start(bf16[10]{0:T(256)(128)(2,1)} %get-tuple-element.33), channel_id=1, source_target_pairs={{4,0},{8,4},{12,8},{16,12},{20,16},{24,20},{28,24},{32,28},{36,32}... | collective-permute-start | bytes 68 | tf_op jit(solution)/shard_map/ppermute | solution.py:15
  35.5 0.7 copy-start.15
  35.5 0.6 copy-start.24
  39.0 2.4 copy-start.2
  39.0 2.4 copy-start.21
  41.4 2.0 copy-start.9
  45.4 9.8 %collective-permute-start.2 = (bf16[10]{0:T(256)(128)(2,1)}, bf16[10]{0:T(256)(128)(2,1)S(1)}, u32[]{:S(2)}, u32[]{:S(2)}) collective-permute-start(bf16[10]{0:T(256)(128)(2,1)} %collective-permute-done), channel_id=1, source_target_pairs={{4,0},{8,4},{12,8},{16,12},{20,16},{24,20},{28,24},{32,28},{36,32}... | collective-permute-start | bytes 68 | tf_op jit(solution)/shard_map/ppermute | solution.py:15
  60.9 12.5 %copy-start.1 = (f32[8,32,10,128]{3,2,1,0:T(8,128)S(1)}, f32[8,32,10,128]{3,2,1,0:T(8,128)}, u32[]{:S(2)}) copy-start(f32[8,32,10,128]{3,2,1,0:T(8,128)} %mul.196) | copy-start | bytes 3932164
  60.9 15.6 %collective-permute-start.3 = (bf16[1280,128]{0,1:T(8,128)(2,1)}, bf16[1280,128]{0,1:T(8,128)(2,1)S(1)}, u32[]{:S(2)}, u32[]{:S(2)}) collective-permute-start(bf16[1280,128]{0,1:T(8,128)(2,1)} %collective-permute-done.1), channel_id=1, source_target_pairs={{4,0},{8,4},{12,8},{16,12},{20,16},{24,20},{28,24},{32,28},{36,32}... | collective-permute-start | bytes 983048 | tf_op jit(solution)/shard_map/ppermute | solution.py:15
  73.4 2.0 copy-start.11
  76.5 0.7 copy-start.19
  81.3 2.4 copy-start.3
  81.3 3.7 copy-start.10
  81.3 3.8 copy-start.12
  81.3 3.8 copy-start.17
  81.3 3.8 copy-start.18
  81.3 3.8 copy-start.23
  83.7 1.8 copy-start.30
  83.7 2.7 copy-start.22
  87.2 1.2 copy-start.27
  92.3 1.3 copy-start.5
  92.3 1.3 copy-start.28
  95.9 14.2 %collective-permute-start.4 = (bf16[1280,128]{0,1:T(8,128)(2,1)S(1)}, bf16[1280,128]{0,1:T(8,128)(2,1)S(1)}, u32[]{:S(2)}, u32[]{:S(2)}) collective-permute-start(bf16[1280,128]{0,1:T(8,128)(2,1)S(1)} %convolution_convert_fusion.1), channel_id=1, source_target_pairs={{508,0},{0,4},{4,8},{8,12},{12,16},{16,20},{20,24},{24,28},{28,32}... | collective-permute-start | bytes 983048 | tf_op jit(solution)/shard_map/ppermute | solution.py:15
  99.6 1.3 copy-start.4
  99.6 1.3 copy-start.26
  100.9 3.4 copy-start.16
  100.9 3.4 copy-start.20
  100.9 3.4 copy-start.25
  104.3 9.1 %copy-start.14 = (bf16[256,768]{1,0:T(8,128)(2,1)S(1)}, bf16[256,768]{1,0:T(8,128)(2,1)}, u32[]{:S(2)}) copy-start(bf16[256,768]{1,0:T(8,128)(2,1)} %param.6) | copy-start | bytes 1179652
  104.3 22.9 %copy-start.7 = (f32[1280,128]{0,1:T(8,128)S(1)}, f32[1280,128]{0,1:T(8,128)}, u32[]{:S(2)}) copy-start(f32[1280,128]{0,1:T(8,128)} %copy-done.6) | copy-start | bytes 1966084
  110.4 16.8 %collective-permute-start.5 = (bf16[1280,128]{0,1:T(8,128)(2,1)S(1)}, bf16[1280,128]{0,1:T(8,128)(2,1)S(1)}, u32[]{:S(2)}, u32[]{:S(2)}) collective-permute-start(bf16[1280,128]{0,1:T(8,128)(2,1)S(1)} %add_convert_fusion), channel_id=1, source_target_pairs={{508,0},{0,4},{4,8},{8,12},{12,16},{16,20},{20,24},{24,28},{28,32}... | collective-permute-start | bytes 983048 | tf_op jit(solution)/shard_map/ppermute | solution.py:15
Sparse Core Ops, SparseCore 0:
  129.0 273.7 all-reduce.1
where the time goes:
time: 412 us
  waiting for transfers between devices  293 us (71%)
  starting transfers between devices  45.4 us (11%)
  other arithmetic  26.7 us (6%)
  local copies, waits for them, and re-layouts  16.6 us (4%)
  matrix products  15.4 us (4%)
  between operations  14.7 us (4%)
    psum x1, waiting for transfers between devices, per_device(): weight_total = lax.psum(query_partial + passage_partial, ('batch', 'mp'))  272 us
    ppermute x6, starting transfers between devices, shifted(): return lax.ppermute(block, axis, route)  45.3 us
    ppermute x6, waiting for transfers between devices, shifted(): return lax.ppermute(block, axis, route)  20.9 us
  transfers between devices with their start and end apart: 7, of which 5 were waited for; matrix products, arithmetic and copies ran while one was open for 6% of the time, Pallas kernels for 0%

commit v1 on v0

--- a/solution.py
+++ b/solution.py
@@ -126,7 +126,7 @@
         passage_pre_grad, projection.T, preferred_element_type=jnp.float32
     ).astype(jnp.bfloat16)
     passage_partial = contract_rows(passage_hidden, passage_pre_grad)
-    weight_total = lax.psum(query_partial + passage_partial, ("batch", "mp"))
+    weight_total = lax.psum(lax.psum(query_partial + passage_partial, "mp"), "batch")
     grad_projection = weight_total / (lax.axis_size("batch") * lax.axis_size("mp"))
     return (losses, grad_query_hidden, grad_passage_hidden, grad_projection)
 

time: 412 us -> 1520 us (3.69)
  the two profiles are of different devices: /device:TPU:1 before, /device:TPU:16 now
where the time goes in v1:
time: 1520 us
  waiting for transfers between devices  1410 us (93%)
  starting transfers between devices  36.9 us (2%)
  other arithmetic  26.7 us (2%)
  local copies, waits for them, and re-layouts  16.6 us (1%)
  matrix products  15.5 us (1%)
    psum x1, waiting for transfers between devices, per_device(): lax.psum(lax.psum(query_partial + passage_partial, 'mp'), 'batch')  1330 us
    psum x1, waiting for transfers between devices, per_device(): lax.psum(query_partial + passage_partial, 'mp')  44.1 us
    ppermute x6, starting transfers between devices, shifted(): return lax.ppermute(block, axis, route)  36.9 us
    ppermute x6, waiting for transfers between devices, shifted(): return lax.ppermute(block, axis, route)  36 us
  transfers between devices with their start and end apart: 8, of which 6 were waited for; matrix products, arithmetic and copies ran while one was open for 2% of the time, Pallas kernels for 0%

profile of v1, /device:TPU:16, one launch (start us, length us, event | category | flops | bytes accessed | tf_op | source)
XLA Modules:
  0.0 1517.7 jit_solution(17414189656046952177)
XLA Ops:
  7.3 1.5 copy-done
  8.7 1.7 multiply_reduce_fusion.1
  10.5 0.9 fusion.16
  11.4 7.6 collective-permute-start.1
  19.0 0.5 convert_convert_fusion
  19.5 11.5 collective-permute-start
  31.0 0.7 fusion.11
  31.7 0.7 fusion.10
  32.3 0.7 iota_compare_fusion.2
  33.1 0.3 multiply_reduce_fusion.6
  33.4 0.6 copy-done.15
  34.1 1.3 convolution_multiply_fusion.2
  35.4 1.6 mul.189
  37.0 2.4 select_reduce_fusion.2
  39.4 2.0 exponential_reduce_fusion.2
  41.4 0.6 bitcast_compare_fusion.2
  41.9 0.6 convert_element_type.72
  42.7 0.6 bitcast_compare_fusion.1
  43.3 4.0 collective-permute-start.2
  47.4 3.7 collective-permute-done.2
  51.3 0.6 bitcast_compare_fusion
  51.9 2.4 convolution_multiply_fusion.1
  54.2 2.7 mul.196
  56.9 7.6 collective-permute-start.3
  64.5 2.2 select_reduce_fusion.1
  66.8 1.9 exponential_reduce_fusion.1
  68.7 5.5 collective-permute-done.3
  74.3 0.7 copy-done.19
  75.0 1.4 convolution_multiply_fusion
  76.4 2.7 mul.200
  79.1 2.4 select_reduce_fusion
  81.5 1.3 exponential_reduce_fusion
  83.3 0.2 select_reduce_fusion.3
  83.5 0.5 fusion.17
  84.3 0.6 div.74
  84.9 0.6 sub.67
  85.5 0.6 mul.210
  86.1 2.0 fusion.7
  88.1 1.3 fusion.18
  89.5 0.6 div.80
  90.1 0.6 sub.71
  90.7 0.6 mul.222
  91.4 2.0 fusion.1
  93.4 0.3 convolution_convert_fusion.1
  93.7 2.6 collective-permute-start.4
  96.3 0.6 div.77
  96.9 0.6 sub.69
  97.5 0.6 mul.216
  98.2 2.0 fusion.4
  100.3 1.4 convolution_add_fusion.2
  101.7 0.4 multiply_reduce_fusion.2
  102.1 7.9 collective-permute-done.4
  110.0 0.3 add_convert_fusion
  110.3 3.5 collective-permute-start.5
  113.8 0.2 fusion.19
  114.1 18.8 %collective-permute-done.5 = bf16[1280,128]{0,1:T(8,128)(2,1)S(1)} collective-permute-done((bf16[1280,128]{0,1:T(8,128)(2,1)S(1)}, bf16[1280,128]{0,1:T(8,128)(2,1)S(1)}, u32[]{:S(2)}, u32[]{:S(2)}) %collective-permute-start.5) | collective-permute-done | bytes 327712 | tf_op jit(solution)/shard_map/ppermute | solution.py:15
  132.9 0.3 multiply_reduce_fusion
  133.3 1.2 fusion.9
  134.6 44.1 %all-reduce.3.cloned.1.call-done = f32[768,128]{0,1:T(8,128)} async-done(((f32[768,128]{0,1:T(8,128)}), f32[768,128]{0,1:T(8,128)}) %all-reduce.3.cloned.1.call-update) | async-done | bytes 393232 | tf_op jit(solution)/shard_map/psum | solution.py:129
  178.8 1.0 convolution_convert_fusion.2
  179.8 2.0 convolution_convert_fusion
  181.8 1327.2 %all-reduce.5.cloned.1.call-done = f32[768,128]{0,1:T(8,128)} async-done(((f32[768,128]{0,1:T(8,128)}), f32[768,128]{0,1:T(8,128)}) %all-reduce.5.cloned.1.call-update) | async-done | bytes 393232 | tf_op jit(solution)/shard_map/psum | solution.py:129
  1509.0 1.0 broadcast_multiply_fusion
  1510.0 0.9 copy.15
  (85 shorter events, 1.7 us)
Async XLA Ops:
  7.2 1.6 copy-start
  7.2 25.9 %copy-start.8 = (bf16[768,128]{1,0:T(8,128)(2,1)S(1)}, bf16[768,128]{1,0:T(8,128)(2,1)}, u32[]{:S(2)}) copy-start(bf16[768,128]{1,0:T(8,128)(2,1)} %param.8) | copy-start | bytes 589828
  7.2 11.8 copy-start.31
  7.2 23.8 %copy-start.29 = (s32[8]{0:T(128)S(1)}, s32[8]{0:T(128)}, u32[]{:S(2)}) copy-start(s32[8]{0:T(128)} %param.9) | copy-start | bytes 100
  7.2 25.9 %copy-start.13 = (bf16[256,768]{1,0:T(8,128)(2,1)S(1)}, bf16[256,768]{1,0:T(8,128)(2,1)}, u32[]{:S(2)}) copy-start(bf16[256,768]{1,0:T(8,128)(2,1)} %param.6) | copy-start | bytes 1179652
  7.2 171.5 %all-reduce.3.cloned.1.call-start = ((), (), s32[]{:S(2)}) async-start(), calls=%async_computation | async-start | bytes 786432 | tf_op jit(solution)/shard_map/psum | solution.py:129
  10.5 22.9 %copy-start.6 = (f32[1280,128]{0,1:T(8,128)}, f32[1280,128]{0,1:T(8,128)S(1)}, u32[]{:S(2)}) copy-start(f32[1280,128]{0,1:T(8,128)S(1)} %get-tuple-element.37) | copy-start | bytes 1966084
  11.4 40.5 %collective-permute-start.1 = (bf16[1280,128]{0,1:T(8,128)(2,1)}, bf16[1280,128]{0,1:T(8,128)(2,1)}, u32[]{:S(2)}, u32[]{:S(2)}) collective-permute-start(bf16[1280,128]{0,1:T(8,128)(2,1)} %fusion.16), channel_id=1, source_target_pairs={{4,0},{8,4},{12,8},{16,12},{20,16},{24,20},{28,24},{32,28},{36,32}... | collective-permute-start | bytes 983048 | tf_op jit(solution)/shard_map/ppermute | solution.py:15
  19.5 22.4 %collective-permute-start = (bf16[10]{0:T(256)(128)(2,1)}, bf16[10]{0:T(256)(128)(2,1)}, u32[]{:S(2)}, u32[]{:S(2)}) collective-permute-start(bf16[10]{0:T(256)(128)(2,1)} %get-tuple-element.33), channel_id=1, source_target_pairs={{4,0},{8,4},{12,8},{16,12},{20,16},{24,20},{28,24},{32,28},{36,32}... | collective-permute-start | bytes 68 | tf_op jit(solution)/shard_map/ppermute | solution.py:15
  33.4 0.7 copy-start.15
  33.4 0.6 copy-start.24
  37.0 2.4 copy-start.2
  37.0 2.4 copy-start.21
  39.4 2.0 copy-start.9
  43.3 7.8 collective-permute-start.2
  56.9 9.9 copy-start.1
  56.9 17.4 %collective-permute-start.3 = (bf16[1280,128]{0,1:T(8,128)(2,1)}, bf16[1280,128]{0,1:T(8,128)(2,1)S(1)}, u32[]{:S(2)}, u32[]{:S(2)}) collective-permute-start(bf16[1280,128]{0,1:T(8,128)(2,1)} %collective-permute-done.1), channel_id=1, source_target_pairs={{4,0},{8,4},{12,8},{16,12},{20,16},{24,20},{28,24},{32,28},{36,32}... | collective-permute-start | bytes 983048 | tf_op jit(solution)/shard_map/ppermute | solution.py:15
  66.8 2.0 copy-start.11
  74.3 0.7 copy-start.19
  79.1 2.4 copy-start.3
  79.1 3.7 copy-start.10
  79.1 3.8 copy-start.12
  79.1 3.8 copy-start.17
  79.1 3.8 copy-start.18
  79.1 3.8 copy-start.23
  81.5 1.8 copy-start.30
  81.5 2.7 copy-start.22
  84.9 1.2 copy-start.27
  90.1 1.3 copy-start.5
  90.1 1.3 copy-start.28
  93.7 16.3 %collective-permute-start.4 = (bf16[1280,128]{0,1:T(8,128)(2,1)S(1)}, bf16[1280,128]{0,1:T(8,128)(2,1)S(1)}, u32[]{:S(2)}, u32[]{:S(2)}) collective-permute-start(bf16[1280,128]{0,1:T(8,128)(2,1)S(1)} %convolution_convert_fusion.1), channel_id=1, source_target_pairs={{508,0},{0,4},{4,8},{8,12},{12,16},{16,20},{20,24},{24,28},{28,32}... | collective-permute-start | bytes 983048 | tf_op jit(solution)/shard_map/ppermute | solution.py:15
  96.9 1.3 copy-start.4
  96.9 1.3 copy-start.26
  98.2 3.4 copy-start.16
  98.2 3.4 copy-start.20
  98.2 3.4 copy-start.25
  100.3 13.6 copy-start.14
  101.7 31.2 %copy-start.7 = (f32[1280,128]{0,1:T(8,128)S(1)}, f32[1280,128]{0,1:T(8,128)}, u32[]{:S(2)}) copy-start(f32[1280,128]{0,1:T(8,128)} %copy-done.6) | copy-start | bytes 1966084
  110.3 22.6 %collective-permute-start.5 = (bf16[1280,128]{0,1:T(8,128)(2,1)S(1)}, bf16[1280,128]{0,1:T(8,128)(2,1)S(1)}, u32[]{:S(2)}, u32[]{:S(2)}) collective-permute-start(bf16[1280,128]{0,1:T(8,128)(2,1)S(1)} %add_convert_fusion), channel_id=1, source_target_pairs={{508,0},{0,4},{4,8},{8,12},{12,16},{16,20},{20,24},{24,28},{28,32}... | collective-permute-start | bytes 983048 | tf_op jit(solution)/shard_map/ppermute | solution.py:15
  134.5 1374.4 %all-reduce.5.cloned.1.call-start = ((), (), s32[]{:S(2)}) async-start(), calls=%async_computation.1 | async-start | bytes 786432 | tf_op jit(solution)/shard_map/psum | solution.py:129
Sparse Core Ops, SparseCore 0:
  134.7 44.0 all-reduce.2
  181.6 1327.2 all-reduce.4
